TPU v7x, 256 devices: a whole 4x4x8 slice. The times are simulated.
256 devices in a mesh: rows: 8 (over z), vocab: 32 (over y, x, core).
Axes of the slice: x: 4, y: 4, z: 8, core: 2. Of those that a mesh axis runs over, the one named last changes fastest.
Arguments:
- hidden: bfloat16 [1024, 8192], P('rows', 'vocab'), may hold values from -30 to 30
- head: bfloat16 [8192, 152064], P(None, ('vocab', 'rows')), may hold values from -1 to 1
- states: int32 [1024], replicated, may hold values from 0 to 2047
- class_of: int32 [152064], P('vocab'), may hold values from 0 to 255, as said below
- table: int32 [2048, 8], replicated, may hold values from -2147483648 to 2147483646, as said below
Outputs:
- log_probs: float32 [1024, 152064], P('rows', 'vocab')
- entropy: float32 [1024], P('rows')
Inputs may be any that keep to these rules, and one draw needn't show every extreme that they name: `class_of`: class 0 is the class of at least one token. `table`: bit 0 of word 0 is set in every state, so class 0 is allowed everywhere.
All inputs are finite; a program needn't handle non-finite values.
Results may differ from a plain program's by a relative error of at most 0.0003.
Values may be sent and summed in bfloat16 or wider, within the bound.
No kernel may reach another device: no remote copies, remote signals or barrier semaphores. Data moves between devices by JAX's collectives and lax.ppermute only.
A program may use at most 128 MiB of HBM per device.

v0:
```python
import jax
import jax.numpy as jnp
from jax import lax
from jax.sharding import PartitionSpec as P

masked_floor = -1e30


def from_everyone(shard, axis):
    copies = jnp.broadcast_to(shard, (lax.axis_size(axis), *shard.shape))
    return lax.all_to_all(copies, axis, split_axis=0, concat_axis=0, tiled=True)


def collected_together(shard, axis):
    leaves = jax.tree.leaves(shard)
    sequence = sorted(range(len(leaves)), key=lambda k: -leaves[k].size)
    width = (1, *leaves[sequence[0]].shape)[-1]
    lines = [
        jnp.pad(leaves[k].reshape(-1), (0, -leaves[k].size % width)).reshape(-1, width)
        for k in sequence
    ]
    both, at, found = (from_everyone(jnp.concatenate(lines), axis), 0, {})
    for k, line in zip(sequence, lines):
        share = both[:, at : at + len(line)].reshape(len(both), -1)
        found[k] = share[:, : leaves[k].size].reshape(-1, *leaves[k].shape)
        at += len(line)
    numbers = iter(range(len(leaves)))
    return jax.tree.map(lambda _: found[next(numbers)], shard)


def combined_pairwise(pieces, combine):
    while len(jax.tree.leaves(pieces)[0]) > 1:
        pieces = jax.vmap(combine)(
            *(jax.tree.map(lambda part: part[side::2], pieces) for side in (0, 1))
        )
    return jax.tree.map(lambda part: part[0], pieces)


def merged(shard, axis, combine):
    pieces = collected_together(shard, axis)
    return combined_pairwise(pieces, combine)


def joined_along(pieces, dim):
    lengths = list(pieces.shape[1:])
    lengths[dim] *= pieces.shape[0]
    return jnp.moveaxis(pieces, 0, dim).reshape(lengths)


def collect(shard, axis, dim):
    pieces = from_everyone(shard, axis)
    return joined_along(pieces, dim)


def token_mask(states, table, class_of):
    words = jnp.take(table, states, axis=0)
    shifts = lax.broadcasted_iota(jnp.int32, (1, 1, 32), 2)
    bit_values = jnp.bitwise_and(jnp.right_shift(words[:, :, None], shifts), 1)
    allowed_class = bit_values.reshape(words.shape[0], words.shape[1] * 32).astype(jnp.bfloat16)
    onehot = (
        lax.broadcasted_iota(jnp.int32, (allowed_class.shape[1], class_of.shape[0]), 0)
        == class_of[None, :]
    ).astype(jnp.bfloat16)
    return jnp.dot(allowed_class, onehot, preferred_element_type=jnp.float32) > 0.5


def masked_peak(logits, allowed):
    return jnp.max(jnp.where(allowed, logits, masked_floor), axis=1)


def weighted_sums(logits, allowed, peak):
    weights = jnp.where(allowed, jnp.exp(logits - peak[:, None]), 0.0)
    return (jnp.sum(weights, axis=1), jnp.sum(weights * logits, axis=1))


def combine(first, second):
    peak = jnp.maximum(first[0], second[0])
    scale_first = jnp.exp(first[0] - peak)
    scale_second = jnp.exp(second[0] - peak)
    return (
        peak,
        first[1] * scale_first + second[1] * scale_second,
        first[2] * scale_first + second[2] * scale_second,
    )


def finish(logits, allowed, peak, total, weighted):
    norm_log = peak + jnp.log(total)
    log_probs = jnp.where(allowed, logits - norm_log[:, None], 0.0)
    return (log_probs, norm_log - weighted / total)


def vocab_stats(logits, allowed):
    peak = masked_peak(logits, allowed)
    total, weighted = weighted_sums(logits, allowed, peak)
    peak, total, weighted = merged((peak, total, weighted), "vocab", combine)
    return (peak, total, weighted)


def on_device(hidden, head, states, class_of, table):
    all_rows = collect(hidden, "rows", 0)
    logits = jnp.dot(
        lax.all_gather(all_rows, "vocab", axis=1, tiled=True),
        head,
        preferred_element_type=jnp.float32,
    )
    group = lax.axis_index("rows")
    own_count = states.shape[0] // lax.axis_size("rows")
    own_logits = lax.all_to_all(logits, "rows", split_axis=0, concat_axis=1, tiled=True)
    own_states = lax.dynamic_slice_in_dim(states, group * own_count, own_count, 0)
    allowed = token_mask(own_states, table, class_of)
    peak, total, weighted = vocab_stats(own_logits, allowed)
    log_probs, entropy = finish(own_logits, allowed, peak, total, weighted)
    return (log_probs, entropy)


def solution(mesh):
    in_specs = (P("rows", "vocab"), P(None, ("vocab", "rows")), P(), P("vocab"), P())
    out_specs = (P("rows", "vocab"), P("rows"))
    return jax.shard_map(
        on_device, mesh=mesh, in_specs=in_specs, out_specs=out_specs, check_vma=False
    )
```

profile of v0, /device:TPU:1, one launch (start us, length us, event | category | flops | bytes accessed | tf_op | source)
XLA Modules:
  0.0 230.6 jit_solution(9323599690425845408)
XLA Ops:
  7.2 0.0 all-gather.2.cloned.1.call-start
  7.2 0.9 broadcast_in_dim.33
  8.1 24.9 %all_to_all.29 = bf16[8,128,256]{2,1,0:T(8,128)(2,1)} all-to-all(bf16[8,128,256]{2,1,0:T(8,128)(2,1)S(1)} %broadcast_in_dim.33), channel_id=1, replica_groups=mesh['rows'=8,'vocab'=32] {'rows'}, dimensions={0} | all-to-all | bytes 1048576 | tf_op jit(solution)/shard_map/all_to_all | solution.py:11
  33.0 0.0 all-gather.2.cloned.1.call-update
  33.0 84.8 %all-gather.2.cloned.1.call-done = bf16[1024,8192]{1,0:T(8,128)(2,1)} async-done(((bf16[1024,256]{1,0:T(8,128)(2,1)}), bf16[1024,8192]{1,0:T(8,128)(2,1)}) %all-gather.2.cloned.1.call-update) | async-done | bytes 16777232 | tf_op jit(solution)/shard_map/all_gather | solution.py:103
  117.8 15.4 %fusion.5 = f32[1024,594]{0,1:T(8,128)S(1)} fusion(bf16[1024,8192]{1,0:T(8,128)(2,1)} %all-gather.2.cloned.1.call-done, bf16[8192,594]{0,1:T(8,128)(2,1)} %param.6), kind=kOutput, calls=%fused_computation.42 | convolution fusion | flops 9965666304 | bytes 28942336 | tf_op jit(solution)/shard_map/dot_general | solution.py:102
  133.2 0.6 copy.19
  133.8 0.2 slice_bitcast_fusion
  133.9 1.9 copy.14
  135.8 6.7 %all-to-all-start.1 = ((f32[8,128,594]{1,2,0:T(8,128)}), f32[8,128,594]{1,2,0:T(8,128)S(1)}, u32[]{:S(2)}, u32[]{:S(2)}) async-start(f32[8,128,594]{1,2,0:T(8,128)} %copy.14), calls=%async_computation.1 | async-start | bytes 4915200 | tf_op jit(solution)/shard_map/all_to_all | solution.py:109
  142.5 0.1 shift_right_arithmetic.23
  142.6 1.2 copy.12
  143.8 0.8 compare_and_fusion
  144.6 1.2 gather_fusion
  145.8 0.9 broadcast_select_fusion
  146.8 0.1 fusion.3
  146.9 55.0 %all-to-all-done.1 = f32[8,128,594]{1,2,0:T(8,128)S(1)} async-done(((f32[8,128,594]{1,2,0:T(8,128)}), f32[8,128,594]{1,2,0:T(8,128)S(1)}, u32[]{:S(2)}, u32[]{:S(2)}) %all-to-all-start.1) | async-done | bytes 2433056 | tf_op jit(solution)/shard_map/all_to_all | solution.py:109
  202.0 0.0 copy-start
  202.0 1.4 copy-done
  203.4 0.0 copy-start.1
  203.4 1.8 all_to_all.24
  205.2 0.0 copy-done.1
  205.2 1.6 select_reduce_fusion
  206.8 0.7 fusion.1
  207.5 13.4 %all_to_all.30 = f32[32,3,128]{2,1,0:T(4,128)S(1)} all-to-all(f32[32,3,128]{2,1,0:T(4,128)S(1)} %broadcast_in_dim.36), channel_id=1, replica_groups=mesh['rows'=8,'vocab'=32] {'vocab'}, dimensions={0} | all-to-all | bytes 98304 | tf_op jit(solution)/shard_map/all_to_all | solution.py:11
  221.5 0.5 bitcast_subtract_fusion
  222.0 1.8 subtract_select_fusion
  (38 shorter events, 0.6 us)
Async XLA Ops:
  7.2 110.6 %all-gather.2.cloned.1.call-start = ((), (), s32[]{:S(2)}) async-start(), calls=%async_computation.3 | async-start | bytes 17301504 | tf_op jit(solution)/shard_map/all_gather | solution.py:103
  135.8 66.1 %all-to-all-start.1 = ((f32[8,128,594]{1,2,0:T(8,128)}), f32[8,128,594]{1,2,0:T(8,128)S(1)}, u32[]{:S(2)}, u32[]{:S(2)}) async-start(f32[8,128,594]{1,2,0:T(8,128)} %copy.14), calls=%async_computation.1 | async-start | bytes 4915200 | tf_op jit(solution)/shard_map/all_to_all | solution.py:109
  202.0 1.4 copy-start
  203.4 1.8 copy-start.1
Sparse Core Ops, SparseCore 0:
  33.1 84.6 all-gather.1
where the time goes:
time: 231 us
  waiting for transfers between devices  140 us (61%)
  blocking collectives  38.3 us (17%)
  matrix products  16.9 us (7%)
  between operations  14.2 us (6%)
  local copies, waits for them, and re-layouts  9.65 us (4%)
  starting transfers between devices  6.77 us (3%)
  other arithmetic  4.96 us (2%)
    all_gather x1, waiting for transfers between devices, on_device(): lax.all_gather(all_rows, 'vocab', axis=1, tiled=True)  84.8 us
    all_to_all x1, waiting for transfers between devices, on_device(): lax.all_to_all(logits, 'rows', split_axis=0, concat_axis=1, tiled=True)  55 us
    all_to_all x2, blocking collectives, from_everyone(): return lax.all_to_all(copies, axis, split_axis=0, concat_axis=0, tiled=True)  38.3 us
    dot_general x1, matrix products, on_device(): jnp.dot(lax.all_gather(all_rows, 'vocab', axis=1, tiled=True), head, pref...  15.4 us
    all_to_all x1, starting transfers between devices, on_device(): lax.all_to_all(logits, 'rows', split_axis=0, concat_axis=1, tiled=True)  6.73 us
  transfers between devices with their start and end apart: 2, of which 2 were waited for; matrix products, arithmetic and copies ran while one was open for 2% of the time, Pallas kernels for 0%

commit v1 on v0

--- a/solution.py
+++ b/solution.py
@@ -100,7 +100,9 @@
 def on_device(hidden, head, states, class_of, table):
     all_rows = collect(hidden, "rows", 0)
     logits = jnp.dot(
-        lax.all_gather(all_rows, "vocab", axis=1, tiled=True),
+        jnp.concatenate(
+            lax.all_to_all(jnp.stack([all_rows] * lax.axis_size("vocab")), "vocab", 0, 0), axis=1
+        ),
         head,
         preferred_element_type=jnp.float32,
     )

time: 231 us -> 381 us (1.65)
  blocking collectives: 38.3 us -> 234 us
  waiting for transfers between devices: 140 us -> 57.4 us
  local copies, waits for them, and re-layouts: 9.65 us -> 62.5 us
  between operations: 14.2 us -> 0.8 us
    all_to_all x0 -> x1, blocking collectives: none -> 195 us  [on_device(): lax.all_to_all(jnp.stack([all_rows] * lax.axis_size('vocab')), 'vocab', 0...]
    all_gather x1 -> x0, waiting for transfers between devices: 84.8 us -> none  [on_device(): lax.all_gather(all_rows, 'vocab', axis=1, tiled=True)]
    reshape x0 -> x1, local copies, waits for them, and re-layouts: none -> 30.7 us  [on_device(): jnp.concatenate(lax.all_to_all(jnp.stack([all_rows] * lax.axis_size('voca...]
    dot_general x0 -> x1, local copies, waits for them, and re-layouts: none -> 25.6 us  [on_device(): jnp.dot(jnp.concatenate(lax.all_to_all(jnp.stack([all_rows] * lax.axis_si...]
  transfers between devices with their start and end apart: 2 -> 1, of which waited for: 2 -> 1; matrix products, arithmetic and copies ran while one was open for 2% -> 1% of each run, Pallas kernels for 0% -> 0%
where the time goes in v1:
time: 381 us; the launch traced here: 380 us
  blocking collectives  234 us (61%)
  local copies, waits for them, and re-layouts  62.5 us (16%)
  waiting for transfers between devices  57.4 us (15%)
  matrix products  17.2 us (5%)
  starting transfers between devices  4.51 us (1%)
  other arithmetic  4.12 us (1%)
    all_to_all x1, blocking collectives, on_device(): lax.all_to_all(jnp.stack([all_rows] * lax.axis_size('vocab')), 'vocab', 0...  195 us
    all_to_all x1, waiting for transfers between devices, on_device(): lax.all_to_all(logits, 'rows', split_axis=0, concat_axis=1, tiled=True)  57.4 us
    all_to_all x2, blocking collectives, from_everyone(): return lax.all_to_all(copies, axis, split_axis=0, concat_axis=0, tiled=True)  38.7 us
    reshape x1, local copies, waits for them, and re-layouts, on_device(): jnp.concatenate(lax.all_to_all(jnp.stack([all_rows] * lax.axis_size('voca...  30.7 us
    dot_general x1, local copies, waits for them, and re-layouts, on_device(): jnp.dot(jnp.concatenate(lax.all_to_all(jnp.stack([all_rows] * lax.axis_si...  25.6 us
    dot_general x1, matrix products, on_device(): jnp.dot(jnp.concatenate(lax.all_to_all(jnp.stack([all_rows] * lax.axis_si...  15.6 us
  transfers between devices with their start and end apart: 1, of which 1 were waited for; matrix products, arithmetic and copies ran while one was open for 1% of the time, Pallas kernels for 0%

profile of v1, /device:TPU:1, one launch (start us, length us, event | category | flops | bytes accessed | tf_op | source)
XLA Modules:
  0.0 380.2 jit_solution(3399105413083209618)
XLA Ops:
  0.6 0.9 broadcast_in_dim.33
  1.5 24.8 %all_to_all.31 = bf16[8,128,256]{2,1,0:T(8,128)(2,1)S(1)} all-to-all(bf16[8,128,256]{2,1,0:T(8,128)(2,1)S(1)} %broadcast_in_dim.33), channel_id=1, replica_groups=mesh['rows'=8,'vocab'=32] {'rows'}, dimensions={0} | all-to-all | bytes 1048576 | tf_op jit(solution)/shard_map/all_to_all | solution.py:11
  26.3 1.9 stack.3
  28.3 195.0 %all_to_all.32 = bf16[32,1024,256]{2,1,0:T(8,128)(2,1)S(1)} all-to-all(bf16[32,1024,256]{2,1,0:T(8,128)(2,1)S(1)} %stack.3), channel_id=1, replica_groups=mesh['rows'=8,'vocab'=32] {'vocab'}, dimensions={0} | all-to-all | bytes 33554432 | tf_op jit(solution)/shard_map/all_to_all | solution.py:104
  223.3 30.7 %copy.12 = bf16[1024,32,256]{2,1,0:T(8,128)(2,1)} copy(bf16[1024,32,256]{2,0,1:T(8,128)(2,1)S(1)} %bitcast.31) | data formatting | bytes 33554432 | tf_op jit(solution)/shard_map/reshape | solution.py:103
  254.0 25.6 %dot_general.9 = bf16[8,128,8192]{2,1,0:T(8,128)(2,1)} reshape(bf16[1024,32,256]{2,1,0:T(8,128)(2,1)} %copy.12) | data formatting | bytes 33554432 | tf_op jit(solution)/shard_map/dot_general | solution.py:102
  279.7 15.6 %fusion = f32[8,128,594]{1,2,0:T(8,128)} fusion(bf16[8,128,8192]{2,1,0:T(8,128)(2,1)} %dot_general.9, bf16[8192,594]{0,1:T(8,128)(2,1)} %param.6), kind=kOutput, calls=%fused_computation.1 | convolution fusion | flops 9965666304 | bytes 28942336 | tf_op jit(solution)/shard_map/dot_general | solution.py:102
  295.3 0.0 copy-start
  295.3 4.5 %all-to-all-start.2 = ((f32[8,128,594]{1,2,0:T(8,128)}), f32[8,128,594]{1,2,0:T(8,128)}, u32[]{:S(2)}, u32[]{:S(2)}) async-start(f32[8,128,594]{1,2,0:T(8,128)} %fusion), calls=%async_computation.2 | async-start | bytes 4915200 | tf_op jit(solution)/shard_map/all_to_all | solution.py:111
  299.8 0.1 shift_right_arithmetic.23
  299.9 0.0 copy-done
  299.9 0.3 copy.10
  300.2 0.8 compare_and_fusion
  301.0 0.6 gather_fusion
  301.7 0.1 broadcast_select_fusion
  301.8 0.1 fusion.5
  301.9 57.4 %all-to-all-done.2 = f32[8,128,594]{1,2,0:T(8,128)} async-done(((f32[8,128,594]{1,2,0:T(8,128)}), f32[8,128,594]{1,2,0:T(8,128)}, u32[]{:S(2)}, u32[]{:S(2)}) %all-to-all-start.2) | async-done | bytes 2433056 | tf_op jit(solution)/shard_map/all_to_all | solution.py:111
  359.3 0.0 copy-start.1
  359.3 1.8 all_to_all.25
  361.1 0.0 copy-done.1
  361.1 1.6 select_reduce_fusion
  362.6 0.7 fusion.3
  363.4 13.9 %all_to_all.33 = f32[32,3,128]{2,1,0:T(4,128)S(1)} all-to-all(f32[32,3,128]{2,1,0:T(4,128)S(1)} %broadcast_in_dim.36), channel_id=1, replica_groups=mesh['rows'=8,'vocab'=32] {'vocab'}, dimensions={0} | all-to-all | bytes 98304 | tf_op jit(solution)/shard_map/all_to_all | solution.py:11
  377.9 0.5 bitcast_subtract_fusion
  378.5 1.8 subtract_select_fusion
  (38 shorter events, 0.6 us)
Async XLA Ops:
  295.3 4.6 %copy-start = (s32[2048,8]{0,1:T(8,128)S(1)}, s32[2048,8]{0,1:T(8,128)}, u32[]{:S(2)}) copy-start(s32[2048,8]{0,1:T(8,128)} %param.9) | copy-start | bytes 196612
  295.3 64.0 %all-to-all-start.2 = ((f32[8,128,594]{1,2,0:T(8,128)}), f32[8,128,594]{1,2,0:T(8,128)}, u32[]{:S(2)}, u32[]{:S(2)}) async-start(f32[8,128,594]{1,2,0:T(8,128)} %fusion), calls=%async_computation.2 | async-start | bytes 4915200 | tf_op jit(solution)/shard_map/all_to_all | solution.py:111
  359.3 1.8 copy-start.1
